TPU v7x, 32 devices: a whole 2x2x4 slice. The times are simulated.
32 devices in a mesh: fsdp: 8 (over y, x, core), rep: 4 (over z).
Axes of the slice: x: 2, y: 2, z: 4, core: 2. Of those that a mesh axis runs over, the one named last changes fastest.
Arguments:
- layer_input: bfloat16 [128, 512, 768], P(('fsdp', 'rep')), may hold values from -6 to 6
- segment_length_pairs: int32 [128, 2], P(('fsdp', 'rep')), may hold values from 16 to 496, as said below
- query_key_value_weight: bfloat16 [3, 768, 768], P(None, 'fsdp', 'rep'), may hold values from -0.21875 to 0.21875
- output_weight: bfloat16 [768, 768], P('fsdp', 'rep'), may hold values from -0.875 to 0.875
- attention_bias: bfloat16 [3, 768], P(None, 'fsdp'), may hold values from -1.5 to 1.5
- adapter_down: bfloat16 [2, 768, 8], P(None, 'fsdp'), may hold values from -0.21875 to 0.21875
- adapter_up: bfloat16 [2, 8, 768], replicated, may hold values from -1 to 1
- layernorm_gain: bfloat16 [2, 768], P(None, 'fsdp'), may hold values from 0.5 to 1.5
- layernorm_bias: bfloat16 [2, 768], P(None, 'fsdp'), may hold values from -1.5 to 1.5
- feedforward_in_weight: bfloat16 [768, 3072], P('fsdp', 'rep'), may hold values from -0.21875 to 0.21875
- feedforward_in_bias: bfloat16 [3072], P('fsdp'), may hold values from -1.5 to 1.5
- feedforward_out_weight: bfloat16 [3072, 768], P('fsdp', 'rep'), may hold values from -0.21875 to 0.21875
- feedforward_out_bias: bfloat16 [768], P('fsdp'), may hold values from -1.5 to 1.5
- output_cotangent: bfloat16 [128, 512, 768], P(('fsdp', 'rep')), may hold values from -6 to 6
Outputs:
- hidden_out: bfloat16 [128, 512, 768], P(('fsdp', 'rep'))
- hidden_grad: bfloat16 [128, 512, 768], P(('fsdp', 'rep'))
- adapter_up_gradient: float32 [2, 8, 768], replicated
Inputs may be any that keep to these rules, and one draw needn't show every extreme that they name: Item i uses slots 0 to segment_length_pairs[i,0] + segment_length_pairs[i,1] - 1 of its 512; that total is at most 512, and exactly 512 for every item whose index is a multiple of 4. The first segment is at most 256. Item 0 has a first segment of 16 and a second of 496; item 1 has a second segment of 16.
All inputs are finite; a program needn't handle non-finite values.
Results may differ from a plain program's by a relative error of at most 0.017.
Values may be sent and summed in bfloat16 or wider, within the bound.
No kernel may reach another device: no remote copies, remote signals or barrier semaphores. Data moves between devices by JAX's collectives and lax.ppermute only.
A program may use at most 320 MiB of HBM per device.

v0:
```python
import math
import jax
import jax.numpy as jnp
from jax import lax
from jax.sharding import PartitionSpec as P

MODEL_WIDTH = 768
H = 12
HD = 64
ADAPTER_RANK = 8
ADAPTER_ALPHA = 16
L = 512
MB = 2


def collect_frozen(frozen_args):
    (
        qkv_part,
        out_part,
        in_part,
        back_part,
        attn_part,
        down_part,
        gain_part,
        shift_part,
        in_bias_part,
        back_bias_part,
    ) = frozen_args
    columns = (
        lax.all_gather(qkv_part, "rep", axis=2, tiled=True),
        lax.all_gather(out_part, "rep", axis=1, tiled=True),
        lax.all_gather(in_part, "rep", axis=1, tiled=True),
        lax.all_gather(back_part, "rep", axis=1, tiled=True),
    )
    return (
        lax.all_gather(columns[0], "fsdp", axis=1, tiled=True),
        lax.all_gather(columns[1], "fsdp", axis=0, tiled=True),
        lax.all_gather(columns[2], "fsdp", axis=0, tiled=True),
        lax.all_gather(columns[3], "fsdp", axis=0, tiled=True),
        lax.all_gather(attn_part, "fsdp", axis=1, tiled=True),
        lax.all_gather(down_part, "fsdp", axis=1, tiled=True),
        lax.all_gather(gain_part, "fsdp", axis=1, tiled=True),
        lax.all_gather(shift_part, "fsdp", axis=1, tiled=True),
        lax.all_gather(in_bias_part, "fsdp", axis=0, tiled=True),
        lax.all_gather(back_bias_part, "fsdp", axis=0, tiled=True),
    )


def adapter_sum(adapter_grad_term):
    return lax.psum(adapter_grad_term, ("fsdp", "rep"))


def exact_gelu(values):
    return jax.nn.gelu(values, approximate=False)


def layer_norm_rows(values):
    centered = values - jnp.mean(values, axis=-1, keepdims=True)
    spread = jnp.mean(centered * centered, axis=-1, keepdims=True)
    inverse = lax.rsqrt(spread + 1e-05)
    return (centered * inverse, inverse)


def norm_back(output_gradient, normed, inverse, gain):
    scaled = output_gradient * gain
    return inverse * (
        scaled
        - jnp.mean(scaled, axis=-1, keepdims=True)
        - normed * jnp.mean(scaled * normed, axis=-1, keepdims=True)
    )


def attention_scores(query_bf, key_bf, valid_keys):
    head_scale = 1.0 / math.sqrt(HD)
    raw_scores = (
        jnp.einsum("ilhe,imhe->ihlm", query_bf, key_bf, preferred_element_type=jnp.float32)
        * head_scale
    )
    return jnp.where(valid_keys[:, None, None, :], raw_scores, -1e30)


def forward_sweep(input_bundle, valid_keys, weight_bundle, adapter_up):
    (
        qkv_full,
        out_full,
        in_full,
        back_full,
        attention_offset,
        down_matrix_whole,
        norm_gains,
        norm_shifts,
        in_shift,
        back_shift,
    ) = weight_bundle
    item_count = valid_keys.shape[0]
    row_count = input_bundle.shape[0]
    adapter_scale = ADAPTER_ALPHA / ADAPTER_RANK
    attention_single = attention_offset.astype(jnp.float32)
    adapter_reduced = jnp.einsum(
        "td,kdr->tkr", input_bundle, down_matrix_whole, preferred_element_type=jnp.float32
    ).astype(jnp.bfloat16)
    projected_rows = jnp.einsum(
        "td,kde->tke", input_bundle, qkv_full, preferred_element_type=jnp.float32
    )
    adapter_term = jnp.einsum(
        "lsn,snb->lsb", adapter_reduced, adapter_up, preferred_element_type=jnp.float32
    )
    head_shape = (item_count, L, H, HD)
    query_bf = (
        (projected_rows[:, 0] + attention_single[0] + adapter_scale * adapter_term[:, 0])
        .astype(jnp.bfloat16)
        .reshape(head_shape)
    )
    key_bf = projected_rows[:, 1].astype(jnp.bfloat16).reshape(head_shape)
    value_bf = (
        (projected_rows[:, 2] + attention_single[1] + adapter_scale * adapter_term[:, 1])
        .astype(jnp.bfloat16)
        .reshape(head_shape)
    )
    scores = attention_scores(query_bf, key_bf, valid_keys)
    row_max = jnp.max(scores, axis=-1, keepdims=True)
    log_total = row_max + jnp.log(jnp.sum(jnp.exp(scores - row_max), axis=-1, keepdims=True))
    probs_bf = jnp.exp(scores - log_total).astype(jnp.bfloat16)
    mixed_bf = (
        jnp.einsum("ihlm,imhe->ilhe", probs_bf, value_bf, preferred_element_type=jnp.float32)
        .astype(jnp.bfloat16)
        .reshape(row_count, MODEL_WIDTH)
    )
    first_sum = (
        input_bundle.astype(jnp.float32)
        + jnp.dot(mixed_bf, out_full, preferred_element_type=jnp.float32)
        + attention_single[2]
    )
    normed_one, inverse_one = layer_norm_rows(first_sum)
    gain_float = norm_gains.astype(jnp.float32)
    shift_float = norm_shifts.astype(jnp.float32)
    hidden_one = normed_one * gain_float[0] + shift_float[0]
    ffn_inner = jnp.dot(
        hidden_one.astype(jnp.bfloat16), in_full, preferred_element_type=jnp.float32
    ) + in_shift.astype(jnp.float32)
    activation = exact_gelu(ffn_inner).astype(jnp.bfloat16)
    second_sum = (
        hidden_one
        + jnp.dot(activation, back_full, preferred_element_type=jnp.float32)
        + back_shift.astype(jnp.float32)
    )
    normed_two, inverse_two = layer_norm_rows(second_sum)
    layer_output = (normed_two * gain_float[1] + shift_float[1]).astype(jnp.bfloat16)
    saved_values = (
        adapter_reduced,
        query_bf,
        key_bf,
        value_bf,
        log_total,
        normed_one,
        inverse_one,
        ffn_inner,
        normed_two,
        inverse_two,
    )
    return (saved_values, layer_output)


def reverse_sweep(output_gradient, saved_values, valid_keys, weight_bundle, adapter_up):
    (
        qkv_full,
        out_full,
        in_full,
        back_full,
        attention_offset,
        down_matrix_whole,
        norm_gains,
        norm_shifts,
        in_shift,
        back_shift,
    ) = weight_bundle
    (
        adapter_reduced,
        query_bf,
        key_bf,
        value_bf,
        log_total,
        normed_one,
        inverse_one,
        ffn_inner,
        normed_two,
        inverse_two,
    ) = saved_values
    item_count = valid_keys.shape[0]
    row_count = output_gradient.shape[0]
    adapter_scale = ADAPTER_ALPHA / ADAPTER_RANK
    head_scale = 1.0 / math.sqrt(HD)
    gain_float = norm_gains.astype(jnp.float32)
    grad_second = norm_back(
        output_gradient.astype(jnp.float32), normed_two, inverse_two, gain_float[1]
    )
    grad_act = jnp.einsum(
        "td,fd->tf", grad_second.astype(jnp.bfloat16), back_full, preferred_element_type=jnp.float32
    )
    gelu_value, gelu_pull = jax.vjp(exact_gelu, ffn_inner)
    grad_inner = gelu_pull(grad_act)[0].astype(jnp.bfloat16)
    grad_hidden = grad_second + jnp.einsum(
        "tf,df->td", grad_inner, in_full, preferred_element_type=jnp.float32
    )
    grad_first = norm_back(grad_hidden, normed_one, inverse_one, gain_float[0])
    grad_mixed = jnp.einsum(
        "td,ed->te", grad_first.astype(jnp.bfloat16), out_full, preferred_element_type=jnp.float32
    )
    grad_mixed = grad_mixed.astype(jnp.bfloat16).reshape(item_count, L, H, HD)
    scores = attention_scores(query_bf, key_bf, valid_keys)
    attn_weights = jnp.exp(scores - log_total)
    probs_bf = attn_weights.astype(jnp.bfloat16)
    grad_probs = jnp.einsum(
        "ilhe,imhe->ihlm", grad_mixed, value_bf, preferred_element_type=jnp.float32
    )
    value_gradient = jnp.einsum(
        "ihlm,ilhe->imhe", probs_bf, grad_mixed, preferred_element_type=jnp.float32
    ).astype(jnp.bfloat16)
    row_inner = jnp.sum(attn_weights * grad_probs, axis=-1, keepdims=True)
    grad_scores = (attn_weights * (grad_probs - row_inner)).astype(jnp.bfloat16)
    query_gradient = (
        jnp.einsum("ihlm,imhe->ilhe", grad_scores, key_bf, preferred_element_type=jnp.float32)
        * head_scale
    ).astype(jnp.bfloat16)
    grad_key = (
        jnp.einsum("ihlm,ilhe->imhe", grad_scores, query_bf, preferred_element_type=jnp.float32)
        * head_scale
    ).astype(jnp.bfloat16)
    query_gradient = query_gradient.reshape(row_count, MODEL_WIDTH)
    grad_key = grad_key.reshape(row_count, MODEL_WIDTH)
    value_gradient = value_gradient.reshape(row_count, MODEL_WIDTH)
    grad_proj = jnp.stack([query_gradient, grad_key, value_gradient], axis=1)
    input_gradient = grad_first + jnp.einsum(
        "tke,kde->td", grad_proj, qkv_full, preferred_element_type=jnp.float32
    )
    adapter_gradient = jnp.stack([query_gradient, value_gradient], axis=1)
    adapter_grad_term = adapter_scale * jnp.einsum(
        "hiu,his->ius", adapter_reduced, adapter_gradient, preferred_element_type=jnp.float32
    )
    grad_u = (
        adapter_scale
        * jnp.einsum(
            "pqf,qnf->pqn", adapter_gradient, adapter_up, preferred_element_type=jnp.float32
        )
    ).astype(jnp.bfloat16)
    input_gradient = input_gradient + jnp.einsum(
        "tkr,kdr->td", grad_u, down_matrix_whole, preferred_element_type=jnp.float32
    )
    return (input_gradient.astype(jnp.bfloat16), adapter_grad_term)


def per_device(
    layer_input,
    segment_length_pairs,
    query_key_value_weight,
    output_weight,
    attention_bias,
    adapter_down,
    adapter_up,
    layernorm_gain,
    layernorm_bias,
    feedforward_in_weight,
    feedforward_in_bias,
    feedforward_out_weight,
    feedforward_out_bias,
    output_cotangent,
):
    frozen_args = (
        query_key_value_weight,
        output_weight,
        feedforward_in_weight,
        feedforward_out_weight,
        attention_bias,
        adapter_down,
        layernorm_gain,
        layernorm_bias,
        feedforward_in_bias,
        feedforward_out_bias,
    )
    per_micro = layer_input.shape[0] // MB
    row_count = per_micro * L
    token_count = layer_input.shape[0] * L * lax.axis_size("fsdp") * lax.axis_size("rep")
    positions = jnp.arange(L, dtype=jnp.int32)
    layer_outputs = []
    input_gradients = []
    gradient_total = jnp.zeros((2, ADAPTER_RANK, MODEL_WIDTH), jnp.float32)
    for micro_index in range(MB):
        weight_bundle = collect_frozen(frozen_args)
        first_item = micro_index * per_micro
        input_bundle = layer_input[first_item : first_item + per_micro].reshape(
            row_count, MODEL_WIDTH
        )
        valid_counts = (
            segment_length_pairs[first_item : first_item + per_micro, 0]
            + segment_length_pairs[first_item : first_item + per_micro, 1]
        )
        valid_keys = positions[None, :] < valid_counts[:, None]
        saved_values, layer_output = forward_sweep(
            input_bundle, valid_keys, weight_bundle, adapter_up
        )
        weight_bundle = collect_frozen(frozen_args)
        gradient_rows = output_cotangent[first_item : first_item + per_micro].reshape(
            row_count, MODEL_WIDTH
        )
        input_gradient, adapter_grad_term = reverse_sweep(
            gradient_rows, saved_values, valid_keys, weight_bundle, adapter_up
        )
        gradient_total = gradient_total + adapter_grad_term
        layer_outputs.append(layer_output.reshape(per_micro, L, MODEL_WIDTH))
        input_gradients.append(input_gradient.reshape(per_micro, L, MODEL_WIDTH))
    gradient_total = adapter_sum(gradient_total)
    adapter_up_gradient = gradient_total / math.sqrt(token_count)
    return (
        jnp.concatenate(layer_outputs, axis=0),
        jnp.concatenate(input_gradients, axis=0),
        adapter_up_gradient,
    )


def solution(mesh):
    in_specs = (
        P(("fsdp", "rep"), None, None),
        P(("fsdp", "rep"), None),
        P(None, "fsdp", "rep"),
        P("fsdp", "rep"),
        P(None, "fsdp"),
        P(None, "fsdp", None),
        P(),
        P(None, "fsdp"),
        P(None, "fsdp"),
        P("fsdp", "rep"),
        P("fsdp"),
        P("fsdp", "rep"),
        P("fsdp"),
        P(("fsdp", "rep"), None, None),
    )
    out_specs = (P(("fsdp", "rep"), None, None), P(("fsdp", "rep"), None, None), P())
    return jax.shard_map(
        per_device, mesh=mesh, in_specs=in_specs, out_specs=out_specs, check_vma=False
    )
```

profile of v0, /device:TPU:0, one launch (start us, length us, event | category | flops | bytes accessed | tf_op | source)
XLA Modules:
  0.0 779.1 jit_solution(15271656868781157294)
XLA Ops:
  8.4 21.9 %all_gather.28 = bf16[3,96,768]{1,0,2:T(4,128)(2,1)} all-gather(bf16[3,96,192]{1,0,2:T(4,128)(2,1)S(1)} %copy.229), channel_id=1, replica_groups=mesh['fsdp'=8,'rep'=4] {'rep'}, dimensions={2}, use_global_device_ids=true | all-gather | bytes 552960 | tf_op jit(solution)/shard_map/all_gather | solution.py:30
  33.4 13.6 %all_gather.32 = bf16[96,768]{0,1:T(8,128)(2,1)S(1)} all-gather(bf16[96,192]{0,1:T(8,128)(2,1)S(1)} %copy.244), channel_id=1, replica_groups=mesh['fsdp'=8,'rep'=4] {'rep'}, dimensions={1}, use_global_device_ids=true | all-gather | bytes 184320 | tf_op jit(solution)/shard_map/all_gather | solution.py:31
  47.8 17.4 %all_gather.36 = bf16[96,3072]{1,0:T(8,128)(2,1)} all-gather(bf16[96,768]{1,0:T(8,128)(2,1)} %param.23), channel_id=1, replica_groups=mesh['fsdp'=8,'rep'=4] {'rep'}, dimensions={1}, use_global_device_ids=true | all-gather | bytes 737280 | tf_op jit(solution)/shard_map/all_gather | solution.py:32
  65.3 16.5 %all_gather.39 = bf16[384,768]{0,1:T(8,128)(2,1)} all-gather(bf16[384,192]{0,1:T(8,128)(2,1)} %param.25), channel_id=1, replica_groups=mesh['fsdp'=8,'rep'=4] {'rep'}, dimensions={1}, use_global_device_ids=true | all-gather | bytes 737280 | tf_op jit(solution)/shard_map/all_gather | solution.py:33
  83.4 12.1 %all-reduce = bf16[768]{0:T(1024)(128)(2,1)S(1)} all-reduce(bf16[768]{0:T(1024)(128)(2,1)S(1)} %dynamic-update-slice), channel_id=1, replica_groups=mesh['fsdp'=8,'rep'=4] {'fsdp'}, use_global_device_ids=true, to_apply=%add | all-reduce | flops 768 | bytes 3072
  96.1 8.7 %all-gather.1 = bf16[8,96,2]{1,2,0:T(2,128)(2,1)S(1)} all-gather(bf16[1,96,2]{1,2,0:T(2,128)(2,1)S(1)} %bitcast.229), channel_id=1, replica_groups=mesh['fsdp'=8,'rep'=4] {'fsdp'}, dimensions={0}, use_global_device_ids=true | all-gather | bytes 3456 | tf_op jit(solution)/shard_map/all_gather | solution.py:42
  104.9 8.1 %all-gather.2 = bf16[8,96,2]{1,2,0:T(2,128)(2,1)S(1)} all-gather(bf16[1,96,2]{1,2,0:T(2,128)(2,1)S(1)} %bitcast.230), channel_id=1, replica_groups=mesh['fsdp'=8,'rep'=4] {'fsdp'}, dimensions={0}, use_global_device_ids=true | all-gather | bytes 3456 | tf_op jit(solution)/shard_map/all_gather | solution.py:43
  113.0 9.0 %all-gather = bf16[8,96,3]{1,2,0:T(4,128)(2,1)S(1)} all-gather(bf16[1,96,3]{1,2,0:T(4,128)(2,1)S(1)} %bitcast.228), channel_id=1, replica_groups=mesh['fsdp'=8,'rep'=4] {'fsdp'}, dimensions={0}, use_global_device_ids=true | all-gather | bytes 5184 | tf_op jit(solution)/shard_map/all_gather | solution.py:40
  124.8 8.2 %all-gather.3 = bf16[8,1,384]{2,1,0:T(2,128)(2,1)S(1)} all-gather(bf16[1,1,384]{2,1,0:T(2,128)(2,1)S(1)} %reshape.269), channel_id=1, replica_groups=mesh['fsdp'=8,'rep'=4] {'fsdp'}, dimensions={0}, use_global_device_ids=true | all-gather | bytes 6912 | tf_op jit(solution)/shard_map/all_gather | solution.py:44
  133.1 9.6 %all_gather.31 = bf16[2,768,8]{2,0,1:T(2,128)(2,1)S(1)} all-gather(bf16[2,96,8]{2,0,1:T(2,128)(2,1)S(1)} %copy.233), channel_id=1, replica_groups=mesh['fsdp'=8,'rep'=4] {'fsdp'}, dimensions={1}, use_global_device_ids=true | all-gather | bytes 27648 | tf_op jit(solution)/shard_map/all_gather | solution.py:41
  252.1 11.1 %fusion = (f32[2,12,512]{2,1,0:T(8,128)S(1)}, f32[2,12,512,512]{2,3,1,0:T(8,128)}) fusion(pred[2,512]{1,0:T(4,128)(4,1)S(1)} %get-tuple-element.62, bf16[2,512,12,64]{1,0,3,2:T(2,128)(2,1)S(1)} %convert_element_type.205, bf16[2,512,12,64]{1,0,3,2:T(2,128)(2,1)S(1)} %get-tuple-element.36), kind=kOutput, calls=%fused_computation.10 | convolution fusion | flops 824168448 | bytes 28361728 | tf_op jit(solution)/shard_map/ilhe,imhe->ihlm/dot_general | solution.py:76
  263.2 12.8 %exponential_reduce_fusion.1 = f32[2,12,512]{2,1,0:T(8,128)S(1)} fusion(f32[2,12,512,512]{2,3,1,0:T(8,128)} %get-tuple-element.45, f32[2,12,512]{2,1,0:T(8,128)S(1)} %get-tuple-element.44, pred[2,512]{1,0:T(4,128)(4,1)S(1)} %get-tuple-element.62), kind=kLoop, calls=%fused_computation.8 | loop fusion | flops 25153536 | bytes 25265152 | tf_op jit(solution)/shard_map/reduce_sum | solution.py:122
  280.5 11.9 %fusion.66 = bf16[2,512,12,64]{1,3,2,0:T(8,128)(2,1)S(1)} fusion(bf16[2,512,12,64]{1,0,3,2:T(2,128)(2,1)S(1)} %get-tuple-element.38, f32[2,12,512,512]{2,3,1,0:T(8,128)} %get-tuple-element.45, f32[2,12,512]{2,1,0:T(8,128)S(1)} %log_add_fusion.1, pred[2,512]{1,0:T(4,128)(4,1)S(1)} %get-tuple-element.62), kind=kOutput, calls=%fused_computation.152 | convolution fusion | flops 831258624 | bytes 28361728 | tf_op jit(solution)/shard_map/ihlm,imhe->ilhe/dot_general | solution.py:125
  301.6 11.1 %fusion.1 = (f32[2,12,512]{2,1,0:T(8,128)S(1)}, f32[2,12,512,512]{2,3,1,0:T(8,128)}) fusion(pred[2,512]{1,0:T(4,128)(4,1)S(1)} %get-tuple-element.61, bf16[2,512,12,64]{1,0,3,2:T(2,128)(2,1)S(1)} %convert_element_type.220, bf16[2,512,12,64]{1,0,3,2:T(2,128)(2,1)S(1)} %copy-done.7), kind=kOutput, calls=%fused_computation.11 | convolution fusion | flops 824168448 | bytes 28361728 | tf_op jit(solution)/shard_map/ilhe,imhe->ihlm/dot_general | solution.py:76
  312.7 11.2 %exponential_reduce_fusion = f32[2,12,512]{2,1,0:T(8,128)S(1)} fusion(f32[2,12,512,512]{2,3,1,0:T(8,128)} %get-tuple-element.43, f32[2,12,512]{2,1,0:T(8,128)S(1)} %get-tuple-element.42, pred[2,512]{1,0:T(4,128)(4,1)S(1)} %get-tuple-element.61), kind=kLoop, calls=%fused_computation.5 | loop fusion | flops 25153536 | bytes 25265152 | tf_op jit(solution)/shard_map/reduce_sum | solution.py:122
  324.0 11.6 %fusion.67 = bf16[2,512,12,64]{1,3,2,0:T(8,128)(2,1)S(1)} fusion(bf16[2,512,12,64]{1,0,3,2:T(2,128)(2,1)S(1)} %copy-done.29, f32[2,12,512,512]{2,3,1,0:T(8,128)} %get-tuple-element.43, f32[2,12,512]{2,1,0:T(8,128)S(1)} %log_add_fusion, pred[2,512]{1,0:T(4,128)(4,1)S(1)} %get-tuple-element.61), kind=kOutput, calls=%fused_computation.153 | convolution fusion | flops 831258624 | bytes 28361728 | tf_op jit(solution)/shard_map/ihlm,imhe->ilhe/dot_general | solution.py:125
  341.6 8.3 %fusion.48 = f32[1024,3072]{1,0:T(8,128)S(1)} fusion(bf16[768,3072]{1,0:T(8,128)(2,1)} %all-gather.13.cloned.1.call-done, f32[1024,768]{1,0:T(8,128)} %copy-done.38, f32[1024]{0:T(1024)S(1)} %add_rsqrt_fusion.1, f32[1024]{0:T(1024)S(1)} %broadcast_multiply_fusion.8, f32[768]{0:T(1024)S(1)} %get-tuple-element.17, f32[768]{0:T(1024)S(1)} %get-tuple-element.63), kind=kOutput, calls=%fused_computation.136 | convolution fusion | flops 4835770368 | bytes 20461568 | tf_op jit(solution)/shard_map/dot_general | solution.py:138
  354.5 59.2 %fusion.4 = (f32[1024,3072]{1,0:T(8,128)}, f32[1024,3072]{1,0:T(8,128)}, f32[1024,3072]{1,0:T(8,128)}) fusion(f32[3072]{0:T(1024)S(1)} %bitcast.223, f32[1024,3072]{1,0:T(8,128)S(1)} %fusion.48, bf16[768,3072]{1,0:T(8,128)(2,1)S(1)} %copy-done.81, f32[1024,768]{1,0:T(8,128)S(1)} %copy-done.35, f32[768]{0:T(1024)S(1)} %get-tuple-element.17, ...), kind=kOutput, calls=%fused_computation.16 | convolution fusion | flops 5232132096 | bytes 58222592 | tf_op jit(solution)/shard_map/dot_general | solution.py:138
  413.7 12.6 %fusion.147 = (f32[1024]{0:T(1024)S(1)}, f32[1024,768]{1,0:T(8,128)S(1)}) fusion(f32[768]{0:T(1024)S(1)} %copy-done.66, bf16[3072,768]{0,1:T(8,128)(2,1)} %all-gather.15.cloned.1.call-done, f32[1024,3072]{1,0:T(8,128)} %get-tuple-element.34, f32[1024,3072]{1,0:T(8,128)} %get-tuple-element.50, f32[3072]{0:T(1024)S(1)} %bitcast.224, ...), kind=kOutput, calls=%fused_computation.262 | convolution fusion | flops 4849925120 | bytes 36209664 | tf_op jit(solution)/shard_map/dot_general | solution.py:144
  427.0 16.0 %fusion.148 = (f32[1024]{0:T(1024)S(1)}, f32[1024,768]{1,0:T(8,128)S(1)}) fusion(f32[768]{0:T(1024)S(1)} %copy-done.66, bf16[3072,768]{0,1:T(8,128)(2,1)} %all-gather.15.cloned.1.call-done, f32[1024,3072]{1,0:T(8,128)} %get-tuple-element.35, f32[1024,3072]{1,0:T(8,128)} %copy-done.88, f32[3072]{0:T(1024)S(1)} %bitcast.225, f32[768]{0:T(1024)S(1)} %get-tuple-element.17, ...), kind=kOutput, calls=%fused_computation.263 | convolution fusion | flops 4849925120 | bytes 36209664 | tf_op jit(solution)/shard_map/dot_general | solution.py:144
  451.9 22.1 %fusion.140 = (f32[1024]{0:T(1024)S(1)}, f32[1024]{0:T(1024)S(1)}, f32[1024,768]{1,0:T(8,128)}) fusion(f32[1024]{0:T(1024)S(1)} %add_rsqrt_fusion.3, f32[1024,768]{1,0:T(8,128)} %copy-done.34, f32[1024]{0:T(1024)S(1)} %broadcast_multiply_fusion.10, f32[768]{0:T(1024)S(1)} %get-tuple-element.63, f32[1024,768]{1,0:T(8,128)} %get-tuple-element.31, ...), kind=kOutput, calls=%fused_computation.255 | convolution fusion | flops 9717151744 | bytes 44071936 | tf_op jit(solution)/shard_map/tf,df->td/dot_general | solution.py:202
  482.9 12.8 %fusion.68 = bf16[2,512,12,64]{1,3,2,0:T(8,128)(2,1)} fusion(bf16[2,512,12,64]{1,0,3,2:T(2,128)(2,1)S(1)} %reshape.254, f32[2,12,512,512]{2,3,1,0:T(8,128)} %get-tuple-element.45, f32[2,12,512]{2,1,0:T(8,128)S(1)} %copy-done.48, pred[2,512]{1,0:T(4,128)(4,1)S(1)} %copy-done.56), kind=kOutput, calls=%fused_computation.154 | convolution fusion | flops 831258624 | bytes 28361728 | tf_op jit(solution)/shard_map/ihlm,ilhe->imhe/dot_general | solution.py:216
  495.7 19.7 %multiply_reduce_fusion.1 = (f32[2,12,512]{2,1,0:T(8,128)S(1)}, f32[2,12,512,512]{2,3,1,0:T(8,128)}) fusion(f32[2,12,512,512]{2,3,1,0:T(8,128)} %get-tuple-element.45, f32[2,12,512]{2,1,0:T(8,128)S(1)} %copy-done.48, pred[2,512]{1,0:T(4,128)(4,1)S(1)} %copy-done.56, bf16[2,512,12,64]{1,0,3,2:T(2,128)(2,1)S(1)} %copy-done.32, ...), kind=kOutput, calls=%fused_computation.3 | convolution fusion | flops 836751360 | bytes 53576704 | tf_op jit(solution)/shard_map/ilhe,imhe->ihlm/dot_general | solution.py:213
  515.4 21.6 %multiply_convert_fusion.1 = bf16[2,12,512,512]{2,3,1,0:T(8,128)(2,1)} fusion(f32[2,12,512,512]{2,3,1,0:T(8,128)} %get-tuple-element.60, f32[2,12,512,512]{2,3,1,0:T(8,128)} %get-tuple-element.45, f32[2,12,512]{2,1,0:T(8,128)S(1)} %get-tuple-element.59, f32[2,12,512]{2,1,0:T(8,128)S(1)} %copy-done.48, pred[2,512]{1,0:T(4,128)(4,1)S(1)} %copy-done.56), kind=kLoop, calls=%fused_computation.2 | loop fusion | flops 37748736 | bytes 63013888 | tf_op jit(solution)/shard_map/convert_element_type | solution.py:220
  537.0 9.9 %fusion.71 = bf16[2,512,12,64]{1,3,2,0:T(8,128)(2,1)} fusion(bf16[2,12,512,512]{2,3,1,0:T(8,128)(2,1)} %multiply_convert_fusion.1, bf16[2,512,12,64]{1,0,3,2:T(2,128)(2,1)S(1)} %copy-done.10), kind=kOutput, calls=%fused_computation.157 | convolution fusion | flops 806879232 | bytes 15728640 | tf_op jit(solution)/shard_map/ihlm,ilhe->imhe/dot_general | solution.py:226
  553.6 22.5 %fusion.141 = (f32[1024]{0:T(1024)S(1)}, f32[1024]{0:T(1024)S(1)}, f32[1024,768]{1,0:T(8,128)}) fusion(f32[1024]{0:T(1024)S(1)} %copy-done.71, f32[1024,768]{1,0:T(8,128)} %copy-done.38, f32[1024]{0:T(1024)S(1)} %copy-done.65, f32[768]{0:T(1024)S(1)} %get-tuple-element.63, f32[1024,768]{1,0:T(8,128)} %get-tuple-element.28, ...), kind=kOutput, calls=%fused_computation.256 | convolution fusion | flops 9717151744 | bytes 44071936 | tf_op jit(solution)/shard_map/tf,df->td/dot_general | solution.py:202
  586.1 12.6 %fusion.69 = bf16[2,512,12,64]{1,3,2,0:T(8,128)(2,1)} fusion(bf16[2,512,12,64]{1,0,3,2:T(2,128)(2,1)} %reshape.256, f32[2,12,512,512]{2,3,1,0:T(8,128)} %get-tuple-element.43, f32[2,12,512]{2,1,0:T(8,128)S(1)} %copy-done.46, pred[2,512]{1,0:T(4,128)(4,1)S(1)} %copy-done.54), kind=kOutput, calls=%fused_computation.155 | convolution fusion | flops 831258624 | bytes 28361728 | tf_op jit(solution)/shard_map/ihlm,ilhe->imhe/dot_general | solution.py:216
  598.7 21.5 %multiply_reduce_fusion = (f32[2,12,512]{2,1,0:T(8,128)S(1)}, f32[2,12,512,512]{2,3,1,0:T(8,128)}) fusion(f32[2,12,512,512]{2,3,1,0:T(8,128)} %get-tuple-element.43, f32[2,12,512]{2,1,0:T(8,128)S(1)} %copy-done.46, pred[2,512]{1,0:T(4,128)(4,1)S(1)} %copy-done.54, bf16[2,512,12,64]{1,0,3,2:T(2,128)(2,1)S(1)} %copy-done.30, bf16[2,512,12,64]{1,0,3,2:T(2,128)(2,1)} %reshape.256), kind=kOutput, calls=%fused_computation.1 | convolution fusion | flops 836751360 | bytes 53576704 | tf_op jit(solution)/shard_map/ilhe,imhe->ihlm/dot_general | solution.py:213
  620.2 21.8 %multiply_convert_fusion = bf16[2,12,512,512]{2,3,1,0:T(8,128)(2,1)} fusion(f32[2,12,512,512]{2,3,1,0:T(8,128)} %get-tuple-element.57, f32[2,12,512,512]{2,3,1,0:T(8,128)} %get-tuple-element.43, f32[2,12,512]{2,1,0:T(8,128)S(1)} %get-tuple-element.56, f32[2,12,512]{2,1,0:T(8,128)S(1)} %copy-done.46, pred[2,512]{1,0:T(4,128)(4,1)S(1)} %copy-done.54), kind=kLoop, calls=%fused_computation | loop fusion | flops 37748736 | bytes 63013888 | tf_op jit(solution)/shard_map/convert_element_type | solution.py:220
  642.1 9.8 %fusion.73 = bf16[2,512,12,64]{1,3,2,0:T(8,128)(2,1)} fusion(bf16[2,12,512,512]{2,3,1,0:T(8,128)(2,1)} %multiply_convert_fusion, bf16[2,512,12,64]{1,0,3,2:T(2,128)(2,1)S(1)} %copy-done.8), kind=kOutput, calls=%fused_computation.159 | convolution fusion | flops 806879232 | bytes 15728640 | tf_op jit(solution)/shard_map/ihlm,ilhe->imhe/dot_general | solution.py:226
  712.4 38.5 %psum.7 = f32[2,8,768]{2,1,0:T(8,128)S(1)} all-reduce(f32[2,8,768]{2,1,0:T(8,128)S(1)} %fusion.101), channel_id=1, replica_groups=mesh['fsdp'=8,'rep'=4] {'fsdp','rep'}, use_global_device_ids=true, to_apply=%region_22.23 | all-reduce | flops 12288 | bytes 98304 | tf_op jit(solution)/shard_map/psum | solution.py:50
  755.5 8.4 %fusion.37 = bf16[1024,768]{1,0:T(8,128)(2,1)S(1)} fusion(f32[1024,768,1]{1,0,2:T(8,128)} %fusion.103, bf16[3,768,768]{2,1,0:T(8,128)(2,1)} %all-gather.9.cloned.1.call-done, bf16[1024,1,768]{2,0,1:T(8,128)(2,1)S(1)} %copy-done.27, bf16[1024,1,768]{2,0,1:T(8,128)(2,1)} %copy.272, bf16[1024,1,768]{2,0,1:T(8,128)(2,1)S(1)} %copy-done.28, ...), kind=kOutput, calls=%fused_computation.83 | convolution fusion | flops 3635675136 | bytes 19283968 | tf_op jit(solution)/shard_map/tke,kde->td/dot_general | solution.py:233
  (316 shorter events, 251.1 us)
Async XLA Ops:
  7.2 140.3 %copy-start = (bf16[2,8,768]{2,1,0:T(8,128)(2,1)S(1)}, bf16[2,8,768]{2,1,0:T(8,128)(2,1)}, u32[]{:S(2)}) copy-start(bf16[2,8,768]{2,1,0:T(8,128)(2,1)} %param.20) | copy-start | bytes 73732
  7.2 173.5 %all-gather.9.cloned.1.call-start = ((), (), s32[]{:S(2)}) async-start(), calls=%async_computation | async-start | bytes 3981312 | tf_op jit(solution)/shard_map/all_gather | solution.py:36
  8.3 73.5 %copy-start.67 = (s32[4,2]{0,1:T(2,128)S(1)}, s32[4,2]{0,1:T(2,128)}, u32[]{:S(2)}) copy-start(s32[4,2]{0,1:T(2,128)} %param.15) | copy-start | bytes 100
  8.3 73.6 %copy-start.78 = (bf16[384]{0:T(512)(128)(2,1)S(1)}, bf16[384]{0:T(512)(128)(2,1)}, u32[]{:S(2)}) copy-start(bf16[384]{0:T(512)(128)(2,1)} %param.24) | copy-start | bytes 2308
  8.3 73.6 %copy-start.87 = (u32[32]{0:T(128)S(1)}, u32[32]{0:T(128)}, u32[]{:S(2)}) copy-start(u32[32]{0:T(128)} %constant.101) | copy-start | bytes 388
  8.3 74.9 %copy-start.86 = (bf16[96]{0:T(256)(128)(2,1)S(1)}, bf16[96]{0:T(256)(128)(2,1)}, u32[]{:S(2)}) copy-start(bf16[96]{0:T(256)(128)(2,1)} %param.26) | copy-start | bytes 580
  8.4 87.8 %copy-start.79 = (bf16[2,96]{1,0:T(2,128)(2,1)S(1)}, bf16[2,96]{1,0:T(2,128)(2,1)}, u32[]{:S(2)}) copy-start(bf16[2,96]{1,0:T(2,128)(2,1)} %param.21) | copy-start | bytes 1156
  8.4 96.5 %copy-start.80 = (bf16[2,96]{1,0:T(2,128)(2,1)S(1)}, bf16[2,96]{1,0:T(2,128)(2,1)}, u32[]{:S(2)}) copy-start(bf16[2,96]{1,0:T(2,128)(2,1)} %param.22) | copy-start | bytes 1156
  8.4 104.6 %copy-start.77 = (bf16[3,96]{1,0:T(4,128)(2,1)S(1)}, bf16[3,96]{1,0:T(4,128)(2,1)}, u32[]{:S(2)}) copy-start(bf16[3,96]{1,0:T(4,128)(2,1)} %param.18) | copy-start | bytes 1732
  8.4 114.5 %copy-start.1 = (bf16[4,512,768]{2,1,0:T(8,128)(2,1)S(1)}, bf16[4,512,768]{2,1,0:T(8,128)(2,1)}, u32[]{:S(2)}) copy-start(bf16[4,512,768]{2,1,0:T(8,128)(2,1)} %param.27) | copy-start | bytes 9437188
  32.4 263.2 %all-gather.11.cloned.1.call-start = ((), (), s32[]{:S(2)}) async-start(), calls=%async_computation.1 | async-start | bytes 1327104 | tf_op jit(solution)/shard_map/all_gather | solution.py:37
  47.8 85.2 %copy-start.76 = (bf16[2,96,8]{1,2,0:T(8,128)(2,1)S(1)}, bf16[2,96,8]{1,2,0:T(8,128)(2,1)}, u32[]{:S(2)}) copy-start(bf16[2,96,8]{1,2,0:T(8,128)(2,1)} %param.19) | copy-start | bytes 9220
  47.8 293.8 %all-gather.13.cloned.1.call-start = ((), (), s32[]{:S(2)}) async-start(), calls=%async_computation.2 | async-start | bytes 5308416 | tf_op jit(solution)/shard_map/all_gather | solution.py:38
  65.3 348.4 %all-gather.15.cloned.1.call-start = ((), (), s32[]{:S(2)}) async-start(), calls=%async_computation.3 | async-start | bytes 5308416 | tf_op jit(solution)/shard_map/all_gather | solution.py:39
  145.7 18.3 %copy-start.51 = (bf16[1024,2,8]{0,2,1:T(8,128)(2,1)}, bf16[1024,2,8]{0,2,1:T(8,128)(2,1)S(1)}, u32[]{:S(2)}) copy-start(bf16[1024,2,8]{0,2,1:T(8,128)(2,1)S(1)} %fusion.99) | copy-start | bytes 98308
  180.7 99.8 %copy-start.55 = (pred[2,512]{1,0:T(4,128)(4,1)}, pred[2,512]{1,0:T(4,128)(4,1)S(1)}, u32[]{:S(2)}) copy-start(pred[2,512]{1,0:T(4,128)(4,1)S(1)} %get-tuple-element.62) | copy-start | bytes 3076
  180.7 143.3 %copy-start.53 = (pred[2,512]{1,0:T(4,128)(4,1)}, pred[2,512]{1,0:T(4,128)(4,1)S(1)}, u32[]{:S(2)}) copy-start(pred[2,512]{1,0:T(4,128)(4,1)S(1)} %get-tuple-element.61) | copy-start | bytes 3076
  210.4 89.1 %copy-start.3 = (bf16[2,512,12,64]{1,0,3,2:T(2,128)(2,1)}, bf16[2,512,12,64]{1,0,3,2:T(2,128)(2,1)S(1)}, u32[]{:S(2)}) copy-start(bf16[2,512,12,64]{1,0,3,2:T(2,128)(2,1)S(1)} %convert_element_type.220) | copy-start | bytes 4718596
  234.5 17.6 %copy-start.5 = (bf16[2,512,12,64]{1,0,3,2:T(2,128)(2,1)}, bf16[2,512,12,64]{1,0,3,2:T(2,128)(2,1)S(1)}, u32[]{:S(2)}) copy-start(bf16[2,512,12,64]{1,0,3,2:T(2,128)(2,1)S(1)} %convert_element_type.205) | copy-start | bytes 4718596
  299.0 175.0 %copy-start.60 = (f32[1024]{0:T(1024)}, f32[1024]{0:T(1024)S(1)}, u32[]{:S(2)}) copy-start(f32[1024]{0:T(1024)S(1)} %broadcast_multiply_fusion.10) | copy-start | bytes 12292
  299.6 174.5 %copy-start.68 = (f32[1024]{0:T(1024)}, f32[1024]{0:T(1024)S(1)}, u32[]{:S(2)}) copy-start(f32[1024]{0:T(1024)S(1)} %add_rsqrt_fusion.3) | copy-start | bytes 12292
  354.5 59.2 %copy-start.66 = (f32[768]{0:T(1024)S(1)}, f32[768]{0:T(1024)}, u32[]{:S(2)}) copy-start(f32[768]{0:T(1024)} %convert_element_type.214) | copy-start | bytes 9220
  451.9 22.8 %copy-start.36 = (f32[1024,768]{1,0:T(8,128)S(1)}, f32[1024,768]{1,0:T(8,128)}, u32[]{:S(2)}) copy-start(f32[1024,768]{1,0:T(8,128)} %copy-done.34) | copy-start | bytes 9437188
  515.4 21.6 %copy-start.10 = (bf16[2,512,12,64]{1,0,3,2:T(2,128)(2,1)S(1)}, bf16[2,512,12,64]{1,0,3,2:T(2,128)(2,1)}, u32[]{:S(2)}) copy-start(bf16[2,512,12,64]{1,0,3,2:T(2,128)(2,1)} %copy-done.9) | copy-start | bytes 4718596
  553.6 22.5 %copy-start.85 = (bf16[768,768]{1,0:T(8,128)(2,1)S(1)}, bf16[768,768]{1,0:T(8,128)(2,1)}, u32[]{:S(2)}) copy-start(bf16[768,768]{1,0:T(8,128)(2,1)} %all-gather.11.cloned.1.call-done) | copy-start | bytes 3538948
  620.2 21.8 %copy-start.8 = (bf16[2,512,12,64]{1,0,3,2:T(2,128)(2,1)S(1)}, bf16[2,512,12,64]{1,0,3,2:T(2,128)(2,1)}, u32[]{:S(2)}) copy-start(bf16[2,512,12,64]{1,0,3,2:T(2,128)(2,1)} %get-tuple-element.37) | copy-start | bytes 4718596
  705.1 48.4 %copy-start.61 = (f32[1024]{0:T(1024)S(1)}, f32[1024]{0:T(1024)}, u32[]{:S(2)}) copy-start(f32[1024]{0:T(1024)} %copy-done.60) | copy-start | bytes 12292
  705.1 48.3 %copy-start.69 = (f32[1024]{0:T(1024)S(1)}, f32[1024]{0:T(1024)}, u32[]{:S(2)}) copy-start(f32[1024]{0:T(1024)} %copy-done.68) | copy-start | bytes 12292
  705.2 48.3 %copy-start.73 = (f32[1024]{0:T(1024)S(1)}, f32[1024]{0:T(1024)}, u32[]{:S(2)}) copy-start(f32[1024]{0:T(1024)} %copy-done.72) | copy-start | bytes 12292
  705.2 48.3 %copy-start.75 = (f32[1024]{0:T(1024)S(1)}, f32[1024]{0:T(1024)}, u32[]{:S(2)}) copy-start(f32[1024]{0:T(1024)} %copy-done.74) | copy-start | bytes 12292
  709.9 41.7 %copy-start.15 = (bf16[1024,768]{1,0:T(8,128)(2,1)S(1)}, bf16[1024,768]{1,0:T(8,128)(2,1)}, u32[]{:S(2)}) copy-start(bf16[1024,768]{1,0:T(8,128)(2,1)} %get-tuple-element.29) | copy-start | bytes 4718596
  709.9 41.7 %copy-start.16 = (bf16[1024,768]{1,0:T(8,128)(2,1)S(1)}, bf16[1024,768]{1,0:T(8,128)(2,1)}, u32[]{:S(2)}) copy-start(bf16[1024,768]{1,0:T(8,128)(2,1)} %get-tuple-element.30) | copy-start | bytes 4718596
  (61 other events, 364.8 us)
Sparse Core Ops, SparseCore 0:
  32.5 33.4 all-gather.8
  67.9 24.0 all-gather.10
  93.9 38.7 all-gather.12
  134.4 39.6 all-gather.14
where the time goes:
time: 784 us; the launch traced here: 779 us
  matrix products  345 us (44%)
  blocking collectives  163 us (21%)
  local copies, waits for them, and re-layouts  154 us (20%)
  other arithmetic  101 us (13%)
  between operations  15.9 us (2%)
    dot_general x2, matrix products, forward_sweep(): jnp.dot(hidden_one.astype(jnp.bfloat16), in_full, preferred_element_type=...  67.6 us
    dot_general x2, matrix products, reverse_sweep(): jnp.einsum('tf,df->td', grad_inner, in_full, preferred_element_type=jnp.f...  44.6 us
    convert_element_type x2, other arithmetic, reverse_sweep(): grad_scores = (attn_weights * (grad_probs - row_inner)).astype(jnp.bfloat16)  43.4 us
    dot_general x2, matrix products, reverse_sweep(): jnp.einsum('ilhe,imhe->ihlm', grad_mixed, value_bf, preferred_element_typ...  41.2 us
    psum x1, blocking collectives, adapter_sum(): return lax.psum(adapter_grad_term, ('fsdp', 'rep'))  38.5 us
    dot_general x2, matrix products, forward_sweep(): jnp.dot(activation, back_full, preferred_element_type=jnp.float32)  28.6 us
    dot_general x2, matrix products, reverse_sweep(): jnp.einsum('ihlm,ilhe->imhe', probs_bf, grad_mixed, preferred_element_typ...  25.4 us
    another operation x12, local copies, waits for them, and re-layouts, reverse_sweep(): grad_proj = jnp.stack([query_gradient, grad_key, value_gradient], axis=1)  24.3 us
  transfers between devices with their start and end apart: 4, of which 0 were waited for; matrix products, arithmetic and copies ran while one was open for 34% of the time, Pallas kernels for 0%

commit v1 on v0

--- a/solution.py
+++ b/solution.py
@@ -11,6 +11,29 @@
 ADAPTER_ALPHA = 16
 L = 512
 MB = 2
+
+
+def store_the_seats_all(shard_in):
+    r1, block_last, placed = (lax.psum(1, "rep"), lax.axis_index("rep"), shard_in.shape[2])
+    heap = list(map(lambda dev_j: (dev_j, (dev_j + 1) % r1), range(r1)))
+    rack = list(map(lambda dev_j: (dev_j, (dev_j - 1) % r1), range(r1)))
+    field_out = jnp.zeros((*shard_in.shape[:2], r1 * placed, *shard_in.shape[3:]), shard_in.dtype)
+    field_out = lax.dynamic_update_slice_in_dim(field_out, shard_in, block_last * placed, axis=2)
+    long_array = found_now = shard_in
+    out_arr = r1 // 2
+    b = 1
+    while b < out_arr + 1:
+        long_array = lax.ppermute(long_array, "rep", heap)
+        field_out = lax.dynamic_update_slice_in_dim(
+            field_out, long_array, (block_last - b) % r1 * placed, axis=2
+        )
+        if b < r1 - out_arr:
+            found_now = lax.ppermute(found_now, "rep", rack)
+            field_out = lax.dynamic_update_slice_in_dim(
+                field_out, found_now, (block_last + b) % r1 * placed, axis=2
+            )
+        b = b + 1
+    return field_out
 
 
 def collect_frozen(frozen_args):
@@ -27,7 +50,7 @@
         back_bias_part,
     ) = frozen_args
     columns = (
-        lax.all_gather(qkv_part, "rep", axis=2, tiled=True),
+        store_the_seats_all(qkv_part),
         lax.all_gather(out_part, "rep", axis=1, tiled=True),
         lax.all_gather(in_part, "rep", axis=1, tiled=True),
         lax.all_gather(back_part, "rep", axis=1, tiled=True),

time: 784 us -> 765 us (0.976)
  blocking collectives: 163 us -> 144 us
  local copies, waits for them, and re-layouts: 154 us -> 144 us
    all_gather x1 -> x0, blocking collectives: 21.9 us -> none  [collect_frozen(): lax.all_gather(qkv_part, 'rep', axis=2, tiled=True)]
    slice x2 -> x0, local copies, waits for them, and re-layouts: 8.27 us -> none  [forward_sweep(): projected_rows[:, 2] + attention_single[1]]
    dynamic_update_slice x0 -> x4, local copies, waits for them, and re-layouts: none -> 8.15 us  [the longest x2 3.76 us: store_the_seats_all(): lax.dynamic_update_slice_in_dim(field_out, long_array, (block_last - b) %...]
    unnamed x189 -> x186, local copies, waits for them, and re-layouts: 21.2 us -> 19.9 us
  transfers between devices with their start and end apart: 4 -> 7, of which waited for: 0 -> 1; matrix products, arithmetic and copies ran while one was open for 34% -> 34% of each run, Pallas kernels for 0% -> 0%
where the time goes in v1:
time: 765 us; the launch traced here: 760 us
  matrix products  345 us (45%)
  local copies, waits for them, and re-layouts  144 us (19%)
  blocking collectives  144 us (19%)
  other arithmetic  101 us (13%)
  between operations  15.9 us (2%)
    dot_general x2, matrix products, forward_sweep(): jnp.dot(hidden_one.astype(jnp.bfloat16), in_full, preferred_element_type=...  67.5 us
    dot_general x2, matrix products, reverse_sweep(): jnp.einsum('tf,df->td', grad_inner, in_full, preferred_element_type=jnp.f...  44.5 us
    convert_element_type x2, other arithmetic, reverse_sweep(): grad_scores = (attn_weights * (grad_probs - row_inner)).astype(jnp.bfloat16)  43.6 us
    dot_general x2, matrix products, reverse_sweep(): jnp.einsum('ilhe,imhe->ihlm', grad_mixed, value_bf, preferred_element_typ...  41.3 us
    psum x1, blocking collectives, adapter_sum(): return lax.psum(adapter_grad_term, ('fsdp', 'rep'))  38.5 us
    dot_general x2, matrix products, forward_sweep(): jnp.dot(activation, back_full, preferred_element_type=jnp.float32)  28.8 us
    dot_general x2, matrix products, reverse_sweep(): jnp.einsum('ihlm,ilhe->imhe', probs_bf, grad_mixed, preferred_element_typ...  25.3 us
    another operation x12, local copies, waits for them, and re-layouts, reverse_sweep(): grad_proj = jnp.stack([query_gradient, grad_key, value_gradient], axis=1)  24.3 us
  transfers between devices with their start and end apart: 7, of which 1 were waited for; matrix products, arithmetic and copies ran while one was open for 34% of the time, Pallas kernels for 0%

profile of v1, /device:TPU:0, one launch (start us, length us, event | category | flops | bytes accessed | tf_op | source)
XLA Modules:
  0.0 759.8 jit_solution(9382113463821285745)
XLA Ops:
  27.3 15.9 %all_gather.29 = bf16[96,768]{0,1:T(8,128)(2,1)S(1)} all-gather(bf16[96,192]{0,1:T(8,128)(2,1)S(1)} %copy.217), channel_id=1, replica_groups=mesh['fsdp'=8,'rep'=4] {'rep'}, dimensions={1}, use_global_device_ids=true | all-gather | bytes 184320 | tf_op jit(solution)/shard_map/all_gather | solution.py:54
  44.1 17.1 %all_gather.33 = bf16[96,3072]{1,0:T(8,128)(2,1)} all-gather(bf16[96,768]{1,0:T(8,128)(2,1)} %param.23), channel_id=1, replica_groups=mesh['fsdp'=8,'rep'=4] {'rep'}, dimensions={1}, use_global_device_ids=true | all-gather | bytes 737280 | tf_op jit(solution)/shard_map/all_gather | solution.py:55
  61.3 16.2 %all_gather.36 = bf16[384,768]{0,1:T(8,128)(2,1)} all-gather(bf16[384,192]{0,1:T(8,128)(2,1)} %param.25), channel_id=1, replica_groups=mesh['fsdp'=8,'rep'=4] {'rep'}, dimensions={1}, use_global_device_ids=true | all-gather | bytes 737280 | tf_op jit(solution)/shard_map/all_gather | solution.py:56
  79.2 12.0 %all-reduce = bf16[768]{0:T(1024)(128)(2,1)S(1)} all-reduce(bf16[768]{0:T(1024)(128)(2,1)S(1)} %dynamic-update-slice), channel_id=1, replica_groups=mesh['fsdp'=8,'rep'=4] {'fsdp'}, use_global_device_ids=true, to_apply=%add | all-reduce | flops 768 | bytes 3072
  91.8 8.9 %all-gather.1 = bf16[8,96,2]{1,2,0:T(2,128)(2,1)S(1)} all-gather(bf16[1,96,2]{1,2,0:T(2,128)(2,1)S(1)} %bitcast.233), channel_id=1, replica_groups=mesh['fsdp'=8,'rep'=4] {'fsdp'}, dimensions={0}, use_global_device_ids=true | all-gather | bytes 3456 | tf_op jit(solution)/shard_map/all_gather | solution.py:65
  100.7 7.8 %all-gather.2 = bf16[8,96,2]{1,2,0:T(2,128)(2,1)S(1)} all-gather(bf16[1,96,2]{1,2,0:T(2,128)(2,1)S(1)} %bitcast.234), channel_id=1, replica_groups=mesh['fsdp'=8,'rep'=4] {'fsdp'}, dimensions={0}, use_global_device_ids=true | all-gather | bytes 3456 | tf_op jit(solution)/shard_map/all_gather | solution.py:66
  108.6 9.2 %all-gather = bf16[8,96,3]{1,2,0:T(4,128)(2,1)S(1)} all-gather(bf16[1,96,3]{1,2,0:T(4,128)(2,1)S(1)} %bitcast.232), channel_id=1, replica_groups=mesh['fsdp'=8,'rep'=4] {'fsdp'}, dimensions={0}, use_global_device_ids=true | all-gather | bytes 5184 | tf_op jit(solution)/shard_map/all_gather | solution.py:63
  120.6 7.9 %all-gather.3 = bf16[8,1,384]{2,1,0:T(2,128)(2,1)S(1)} all-gather(bf16[1,1,384]{2,1,0:T(2,128)(2,1)S(1)} %reshape.269), channel_id=1, replica_groups=mesh['fsdp'=8,'rep'=4] {'fsdp'}, dimensions={0}, use_global_device_ids=true | all-gather | bytes 6912 | tf_op jit(solution)/shard_map/all_gather | solution.py:67
  128.7 10.2 %all_gather.28 = bf16[2,768,8]{2,0,1:T(2,128)(2,1)S(1)} all-gather(bf16[2,96,8]{2,0,1:T(2,128)(2,1)S(1)} %copy.208), channel_id=1, replica_groups=mesh['fsdp'=8,'rep'=4] {'fsdp'}, dimensions={1}, use_global_device_ids=true | all-gather | bytes 27648 | tf_op jit(solution)/shard_map/all_gather | solution.py:64
  224.6 7.9 %add_convert_fusion.8 = (bf16[2,512,12,64]{1,0,3,2:T(2,128)(2,1)S(1)}, bf16[2,512,12,64]{1,0,3,2:T(2,128)(2,1)}) fusion(f32[2,512,12,64]{1,0,3,2:T(2,128)} %mul.341, f32[2,512,12,64]{1,0,3,2:T(2,128)} %squeeze.9, f32[12,64]{1,0:T(8,128)S(1)} %add.284, f32[2,512,12,64]{1,0,3,2:T(2,128)} %mul.361, f32[2,512,12,64]{1,0,3,2:T(2,128)} %squeeze.11), kind=kLoop, calls=%fused_computation.118 | loop fusion | flops 4718592 | bytes 15731712 | tf_op jit(solution)/shard_map/convert_element_type | solution.py:134
  232.6 11.1 %fusion = (f32[2,12,512]{2,1,0:T(8,128)S(1)}, f32[2,12,512,512]{2,3,1,0:T(8,128)}) fusion(pred[2,512]{1,0:T(4,128)(4,1)S(1)} %get-tuple-element.62, bf16[2,512,12,64]{1,0,3,2:T(2,128)(2,1)S(1)} %convert_element_type.205, bf16[2,512,12,64]{1,0,3,2:T(2,128)(2,1)S(1)} %get-tuple-element.36), kind=kOutput, calls=%fused_computation.10 | convolution fusion | flops 824168448 | bytes 28361728 | tf_op jit(solution)/shard_map/ilhe,imhe->ihlm/dot_general | solution.py:99
  243.7 12.8 %exponential_reduce_fusion.1 = f32[2,12,512]{2,1,0:T(8,128)S(1)} fusion(f32[2,12,512,512]{2,3,1,0:T(8,128)} %get-tuple-element.45, f32[2,12,512]{2,1,0:T(8,128)S(1)} %get-tuple-element.44, pred[2,512]{1,0:T(4,128)(4,1)S(1)} %get-tuple-element.62), kind=kLoop, calls=%fused_computation.8 | loop fusion | flops 25153536 | bytes 25265152 | tf_op jit(solution)/shard_map/reduce_sum | solution.py:145
  261.0 12.2 %fusion.66 = bf16[2,512,12,64]{1,3,2,0:T(8,128)(2,1)S(1)} fusion(bf16[2,512,12,64]{1,0,3,2:T(2,128)(2,1)S(1)} %get-tuple-element.38, f32[2,12,512,512]{2,3,1,0:T(8,128)} %get-tuple-element.45, f32[2,12,512]{2,1,0:T(8,128)S(1)} %log_add_fusion.1, pred[2,512]{1,0:T(4,128)(4,1)S(1)} %get-tuple-element.62), kind=kOutput, calls=%fused_computation.154 | convolution fusion | flops 831258624 | bytes 28361728 | tf_op jit(solution)/shard_map/ihlm,imhe->ilhe/dot_general | solution.py:148
  282.4 11.1 %fusion.1 = (f32[2,12,512]{2,1,0:T(8,128)S(1)}, f32[2,12,512,512]{2,3,1,0:T(8,128)}) fusion(pred[2,512]{1,0:T(4,128)(4,1)S(1)} %get-tuple-element.61, bf16[2,512,12,64]{1,0,3,2:T(2,128)(2,1)S(1)} %convert_element_type.220, bf16[2,512,12,64]{1,0,3,2:T(2,128)(2,1)S(1)} %copy-done.7), kind=kOutput, calls=%fused_computation.11 | convolution fusion | flops 824168448 | bytes 28361728 | tf_op jit(solution)/shard_map/ilhe,imhe->ihlm/dot_general | solution.py:99
  293.5 11.2 %exponential_reduce_fusion = f32[2,12,512]{2,1,0:T(8,128)S(1)} fusion(f32[2,12,512,512]{2,3,1,0:T(8,128)} %get-tuple-element.43, f32[2,12,512]{2,1,0:T(8,128)S(1)} %get-tuple-element.42, pred[2,512]{1,0:T(4,128)(4,1)S(1)} %get-tuple-element.61), kind=kLoop, calls=%fused_computation.5 | loop fusion | flops 25153536 | bytes 25265152 | tf_op jit(solution)/shard_map/reduce_sum | solution.py:145
  304.8 11.3 %fusion.67 = bf16[2,512,12,64]{1,3,2,0:T(8,128)(2,1)S(1)} fusion(bf16[2,512,12,64]{1,0,3,2:T(2,128)(2,1)S(1)} %copy-done.28, f32[2,12,512,512]{2,3,1,0:T(8,128)} %get-tuple-element.43, f32[2,12,512]{2,1,0:T(8,128)S(1)} %log_add_fusion, pred[2,512]{1,0:T(4,128)(4,1)S(1)} %get-tuple-element.61), kind=kOutput, calls=%fused_computation.155 | convolution fusion | flops 831258624 | bytes 28361728 | tf_op jit(solution)/shard_map/ihlm,imhe->ilhe/dot_general | solution.py:148
  322.1 8.3 %fusion.48 = f32[1024,3072]{1,0:T(8,128)S(1)} fusion(bf16[768,3072]{1,0:T(8,128)(2,1)} %all-gather.13.cloned.1.call-done, f32[1024,768]{1,0:T(8,128)} %copy-done.37, f32[1024]{0:T(1024)S(1)} %add_rsqrt_fusion.1, f32[1024]{0:T(1024)S(1)} %broadcast_multiply_fusion.8, f32[768]{0:T(1024)S(1)} %get-tuple-element.17, f32[768]{0:T(1024)S(1)} %get-tuple-element.63), kind=kOutput, calls=%fused_computation.138 | convolution fusion | flops 4835770368 | bytes 20461568 | tf_op jit(solution)/shard_map/dot_general | solution.py:161
  335.0 59.2 %fusion.4 = (f32[1024,3072]{1,0:T(8,128)}, f32[1024,3072]{1,0:T(8,128)}, f32[1024,3072]{1,0:T(8,128)}) fusion(f32[3072]{0:T(1024)S(1)} %bitcast.227, f32[1024,3072]{1,0:T(8,128)S(1)} %fusion.48, bf16[768,3072]{1,0:T(8,128)(2,1)S(1)} %copy-done.80, f32[1024,768]{1,0:T(8,128)S(1)} %copy-done.34, f32[768]{0:T(1024)S(1)} %get-tuple-element.17, ...), kind=kOutput, calls=%fused_computation.16 | convolution fusion | flops 5232132096 | bytes 58222592 | tf_op jit(solution)/shard_map/dot_general | solution.py:161
  394.2 12.5 %fusion.147 = (f32[1024]{0:T(1024)S(1)}, f32[1024,768]{1,0:T(8,128)S(1)}) fusion(f32[768]{0:T(1024)S(1)} %copy-done.65, bf16[3072,768]{0,1:T(8,128)(2,1)} %all-gather.15.cloned.1.call-done, f32[1024,3072]{1,0:T(8,128)} %get-tuple-element.34, f32[1024,3072]{1,0:T(8,128)} %get-tuple-element.50, f32[3072]{0:T(1024)S(1)} %bitcast.228, ...), kind=kOutput, calls=%fused_computation.264 | convolution fusion | flops 4849925120 | bytes 36209664 | tf_op jit(solution)/shard_map/dot_general | solution.py:167
  407.5 16.3 %fusion.148 = (f32[1024]{0:T(1024)S(1)}, f32[1024,768]{1,0:T(8,128)S(1)}) fusion(f32[768]{0:T(1024)S(1)} %copy-done.65, bf16[3072,768]{0,1:T(8,128)(2,1)} %all-gather.15.cloned.1.call-done, f32[1024,3072]{1,0:T(8,128)} %get-tuple-element.35, f32[1024,3072]{1,0:T(8,128)} %copy-done.87, f32[3072]{0:T(1024)S(1)} %bitcast.229, f32[768]{0:T(1024)S(1)} %get-tuple-element.17, ...), kind=kOutput, calls=%fused_computation.265 | convolution fusion | flops 4849925120 | bytes 36209664 | tf_op jit(solution)/shard_map/dot_general | solution.py:167
  432.6 22.2 %fusion.140 = (f32[1024]{0:T(1024)S(1)}, f32[1024]{0:T(1024)S(1)}, f32[1024,768]{1,0:T(8,128)}) fusion(f32[1024]{0:T(1024)S(1)} %add_rsqrt_fusion.3, f32[1024,768]{1,0:T(8,128)} %copy-done.33, f32[1024]{0:T(1024)S(1)} %broadcast_multiply_fusion.10, f32[768]{0:T(1024)S(1)} %get-tuple-element.63, f32[1024,768]{1,0:T(8,128)} %get-tuple-element.31, ...), kind=kOutput, calls=%fused_computation.257 | convolution fusion | flops 9717151744 | bytes 44071936 | tf_op jit(solution)/shard_map/tf,df->td/dot_general | solution.py:225
  463.7 12.7 %fusion.68 = bf16[2,512,12,64]{1,3,2,0:T(8,128)(2,1)} fusion(bf16[2,512,12,64]{1,0,3,2:T(2,128)(2,1)S(1)} %reshape.254, f32[2,12,512,512]{2,3,1,0:T(8,128)} %get-tuple-element.45, f32[2,12,512]{2,1,0:T(8,128)S(1)} %copy-done.47, pred[2,512]{1,0:T(4,128)(4,1)S(1)} %copy-done.55), kind=kOutput, calls=%fused_computation.156 | convolution fusion | flops 831258624 | bytes 28361728 | tf_op jit(solution)/shard_map/ihlm,ilhe->imhe/dot_general | solution.py:239
  476.4 19.7 %multiply_reduce_fusion.1 = (f32[2,12,512]{2,1,0:T(8,128)S(1)}, f32[2,12,512,512]{2,3,1,0:T(8,128)}) fusion(f32[2,12,512,512]{2,3,1,0:T(8,128)} %get-tuple-element.45, f32[2,12,512]{2,1,0:T(8,128)S(1)} %copy-done.47, pred[2,512]{1,0:T(4,128)(4,1)S(1)} %copy-done.55, bf16[2,512,12,64]{1,0,3,2:T(2,128)(2,1)S(1)} %copy-done.31, ...), kind=kOutput, calls=%fused_computation.3 | convolution fusion | flops 836751360 | bytes 53576704 | tf_op jit(solution)/shard_map/ilhe,imhe->ihlm/dot_general | solution.py:236
  496.2 21.6 %multiply_convert_fusion.1 = bf16[2,12,512,512]{2,3,1,0:T(8,128)(2,1)} fusion(f32[2,12,512,512]{2,3,1,0:T(8,128)} %get-tuple-element.60, f32[2,12,512,512]{2,3,1,0:T(8,128)} %get-tuple-element.45, f32[2,12,512]{2,1,0:T(8,128)S(1)} %get-tuple-element.59, f32[2,12,512]{2,1,0:T(8,128)S(1)} %copy-done.47, pred[2,512]{1,0:T(4,128)(4,1)S(1)} %copy-done.55), kind=kLoop, calls=%fused_computation.2 | loop fusion | flops 37748736 | bytes 63013888 | tf_op jit(solution)/shard_map/convert_element_type | solution.py:243
  517.8 9.9 %fusion.71 = bf16[2,512,12,64]{1,3,2,0:T(8,128)(2,1)} fusion(bf16[2,12,512,512]{2,3,1,0:T(8,128)(2,1)} %multiply_convert_fusion.1, bf16[2,512,12,64]{1,0,3,2:T(2,128)(2,1)S(1)} %copy-done.10), kind=kOutput, calls=%fused_computation.159 | convolution fusion | flops 806879232 | bytes 15728640 | tf_op jit(solution)/shard_map/ihlm,ilhe->imhe/dot_general | solution.py:249
  534.4 22.3 %fusion.141 = (f32[1024]{0:T(1024)S(1)}, f32[1024]{0:T(1024)S(1)}, f32[1024,768]{1,0:T(8,128)}) fusion(f32[1024]{0:T(1024)S(1)} %copy-done.70, f32[1024,768]{1,0:T(8,128)} %copy-done.37, f32[1024]{0:T(1024)S(1)} %copy-done.63, f32[768]{0:T(1024)S(1)} %get-tuple-element.63, f32[1024,768]{1,0:T(8,128)} %get-tuple-element.28, ...), kind=kOutput, calls=%fused_computation.258 | convolution fusion | flops 9717151744 | bytes 44071936 | tf_op jit(solution)/shard_map/tf,df->td/dot_general | solution.py:225
  566.7 12.6 %fusion.69 = bf16[2,512,12,64]{1,3,2,0:T(8,128)(2,1)} fusion(bf16[2,512,12,64]{1,0,3,2:T(2,128)(2,1)} %reshape.256, f32[2,12,512,512]{2,3,1,0:T(8,128)} %get-tuple-element.43, f32[2,12,512]{2,1,0:T(8,128)S(1)} %copy-done.45, pred[2,512]{1,0:T(4,128)(4,1)S(1)} %copy-done.53), kind=kOutput, calls=%fused_computation.157 | convolution fusion | flops 831258624 | bytes 28361728 | tf_op jit(solution)/shard_map/ihlm,ilhe->imhe/dot_general | solution.py:239
  579.3 21.5 %multiply_reduce_fusion = (f32[2,12,512]{2,1,0:T(8,128)S(1)}, f32[2,12,512,512]{2,3,1,0:T(8,128)}) fusion(f32[2,12,512,512]{2,3,1,0:T(8,128)} %get-tuple-element.43, f32[2,12,512]{2,1,0:T(8,128)S(1)} %copy-done.45, pred[2,512]{1,0:T(4,128)(4,1)S(1)} %copy-done.53, bf16[2,512,12,64]{1,0,3,2:T(2,128)(2,1)S(1)} %copy-done.29, bf16[2,512,12,64]{1,0,3,2:T(2,128)(2,1)} %reshape.256), kind=kOutput, calls=%fused_computation.1 | convolution fusion | flops 836751360 | bytes 53576704 | tf_op jit(solution)/shard_map/ilhe,imhe->ihlm/dot_general | solution.py:236
  600.8 22.0 %multiply_convert_fusion = bf16[2,12,512,512]{2,3,1,0:T(8,128)(2,1)} fusion(f32[2,12,512,512]{2,3,1,0:T(8,128)} %get-tuple-element.57, f32[2,12,512,512]{2,3,1,0:T(8,128)} %get-tuple-element.43, f32[2,12,512]{2,1,0:T(8,128)S(1)} %get-tuple-element.56, f32[2,12,512]{2,1,0:T(8,128)S(1)} %copy-done.45, pred[2,512]{1,0:T(4,128)(4,1)S(1)} %copy-done.53), kind=kLoop, calls=%fused_computation | loop fusion | flops 37748736 | bytes 63013888 | tf_op jit(solution)/shard_map/convert_element_type | solution.py:243
  622.9 9.8 %fusion.73 = bf16[2,512,12,64]{1,3,2,0:T(8,128)(2,1)} fusion(bf16[2,12,512,512]{2,3,1,0:T(8,128)(2,1)} %multiply_convert_fusion, bf16[2,512,12,64]{1,0,3,2:T(2,128)(2,1)S(1)} %copy-done.8), kind=kOutput, calls=%fused_computation.161 | convolution fusion | flops 806879232 | bytes 15728640 | tf_op jit(solution)/shard_map/ihlm,ilhe->imhe/dot_general | solution.py:249
  693.2 38.5 %psum.7 = f32[2,8,768]{2,1,0:T(8,128)S(1)} all-reduce(f32[2,8,768]{2,1,0:T(8,128)S(1)} %fusion.101), channel_id=1, replica_groups=mesh['fsdp'=8,'rep'=4] {'fsdp','rep'}, use_global_device_ids=true, to_apply=%region_22.23 | all-reduce | flops 12288 | bytes 98304 | tf_op jit(solution)/shard_map/psum | solution.py:73
  736.4 8.4 %fusion.37 = bf16[1024,768]{1,0:T(8,128)(2,1)S(1)} fusion(f32[1024,768,1]{1,0,2:T(8,128)} %fusion.103, bf16[3,768,768]{2,1,0:T(8,128)(2,1)} %all-gather.9.cloned.1.call-done, bf16[1024,1,768]{2,0,1:T(8,128)(2,1)S(1)} %copy-done.26, bf16[1024,1,768]{2,0,1:T(8,128)(2,1)} %copy.242, bf16[1024,1,768]{2,0,1:T(8,128)(2,1)S(1)} %copy-done.27, ...), kind=kOutput, calls=%fused_computation.85 | convolution fusion | flops 3635675136 | bytes 19283968 | tf_op jit(solution)/shard_map/tke,kde->td/dot_general | solution.py:256
  (316 shorter events, 243.3 us)
Async XLA Ops:
  7.2 136.5 %copy-start = (bf16[2,8,768]{2,1,0:T(8,128)(2,1)S(1)}, bf16[2,8,768]{2,1,0:T(8,128)(2,1)}, u32[]{:S(2)}) copy-start(bf16[2,8,768]{2,1,0:T(8,128)(2,1)} %param.20) | copy-start | bytes 73732
  7.2 70.5 %copy-start.86 = (u32[32]{0:T(128)S(1)}, u32[32]{0:T(128)}, u32[]{:S(2)}) copy-start(u32[32]{0:T(128)} %constant.158) | copy-start | bytes 388
  7.2 70.4 %copy-start.66 = (s32[4,2]{0,1:T(2,128)S(1)}, s32[4,2]{0,1:T(2,128)}, u32[]{:S(2)}) copy-start(s32[4,2]{0,1:T(2,128)} %param.15) | copy-start | bytes 100
  7.2 70.4 %copy-start.77 = (bf16[384]{0:T(512)(128)(2,1)S(1)}, bf16[384]{0:T(512)(128)(2,1)}, u32[]{:S(2)}) copy-start(bf16[384]{0:T(512)(128)(2,1)} %param.24) | copy-start | bytes 2308
  7.2 71.7 %copy-start.85 = (bf16[96]{0:T(256)(128)(2,1)S(1)}, bf16[96]{0:T(256)(128)(2,1)}, u32[]{:S(2)}) copy-start(bf16[96]{0:T(256)(128)(2,1)} %param.26) | copy-start | bytes 580
  7.2 84.5 %copy-start.78 = (bf16[2,96]{1,0:T(2,128)(2,1)S(1)}, bf16[2,96]{1,0:T(2,128)(2,1)}, u32[]{:S(2)}) copy-start(bf16[2,96]{1,0:T(2,128)(2,1)} %param.21) | copy-start | bytes 1156
  7.2 93.5 %copy-start.79 = (bf16[2,96]{1,0:T(2,128)(2,1)S(1)}, bf16[2,96]{1,0:T(2,128)(2,1)}, u32[]{:S(2)}) copy-start(bf16[2,96]{1,0:T(2,128)(2,1)} %param.22) | copy-start | bytes 1156
  7.2 101.4 %copy-start.76 = (bf16[3,96]{1,0:T(4,128)(2,1)S(1)}, bf16[3,96]{1,0:T(4,128)(2,1)}, u32[]{:S(2)}) copy-start(bf16[3,96]{1,0:T(4,128)(2,1)} %param.18) | copy-start | bytes 1732
  7.3 111.5 %copy-start.1 = (bf16[4,512,768]{2,1,0:T(8,128)(2,1)S(1)}, bf16[4,512,768]{2,1,0:T(8,128)(2,1)}, u32[]{:S(2)}) copy-start(bf16[4,512,768]{2,1,0:T(8,128)(2,1)} %param.27) | copy-start | bytes 9437188
  7.3 169.6 %all-gather.9.cloned.1.call-start = ((), (), s32[]{:S(2)}) async-start(), calls=%async_computation | async-start | bytes 3981312 | tf_op jit(solution)/shard_map/all_gather | solution.py:59
  7.3 10.1 %collective-permute-start = (bf16[3,96,192]{2,1,0:T(8,128)(2,1)}, bf16[3,96,192]{2,1,0:T(8,128)(2,1)S(1)}, u32[]{:S(2)}, u32[]{:S(2)}) collective-permute-start(bf16[3,96,192]{2,1,0:T(8,128)(2,1)} %param.16), channel_id=1, source_target_pairs={{0,1},{1,2},{2,3},{3,0},{4,5},{5,6},{6,7},{7,4},{8,9},{9,10},{10,1... | collective-permute-start | bytes 331784 | tf_op jit(solution)/shard_map/ppermute | solution.py:26
  10.4 11.7 %collective-permute-start.1 = (bf16[3,96,192]{2,1,0:T(8,128)(2,1)}, bf16[3,96,192]{2,1,0:T(8,128)(2,1)}, u32[]{:S(2)}, u32[]{:S(2)}) collective-permute-start(bf16[3,96,192]{2,1,0:T(8,128)(2,1)} %param.16), channel_id=1, source_target_pairs={{0,3},{1,0},{2,1},{3,2},{4,7},{5,4},{6,5},{7,6},{8,11},{9,8},{10,9... | collective-permute-start | bytes 331784 | tf_op jit(solution)/shard_map/ppermute | solution.py:31
  17.4 7.2 collective-permute-start.2
  26.4 250.0 %all-gather.11.cloned.1.call-start = ((), (), s32[]{:S(2)}) async-start(), calls=%async_computation.1 | async-start | bytes 1327104 | tf_op jit(solution)/shard_map/all_gather | solution.py:60
  44.0 84.6 %copy-start.75 = (bf16[2,96,8]{1,2,0:T(8,128)(2,1)S(1)}, bf16[2,96,8]{1,2,0:T(8,128)(2,1)}, u32[]{:S(2)}) copy-start(bf16[2,96,8]{1,2,0:T(8,128)(2,1)} %param.19) | copy-start | bytes 9220
  44.1 278.1 %all-gather.13.cloned.1.call-start = ((), (), s32[]{:S(2)}) async-start(), calls=%async_computation.2 | async-start | bytes 5308416 | tf_op jit(solution)/shard_map/all_gather | solution.py:61
  61.3 333.0 %all-gather.15.cloned.1.call-start = ((), (), s32[]{:S(2)}) async-start(), calls=%async_computation.3 | async-start | bytes 5308416 | tf_op jit(solution)/shard_map/all_gather | solution.py:62
  176.8 84.2 %copy-start.54 = (pred[2,512]{1,0:T(4,128)(4,1)}, pred[2,512]{1,0:T(4,128)(4,1)S(1)}, u32[]{:S(2)}) copy-start(pred[2,512]{1,0:T(4,128)(4,1)S(1)} %get-tuple-element.62) | copy-start | bytes 3076
  176.8 127.9 %copy-start.52 = (pred[2,512]{1,0:T(4,128)(4,1)}, pred[2,512]{1,0:T(4,128)(4,1)S(1)}, u32[]{:S(2)}) copy-start(pred[2,512]{1,0:T(4,128)(4,1)S(1)} %get-tuple-element.61) | copy-start | bytes 3076
  198.0 82.4 %copy-start.3 = (bf16[2,512,12,64]{1,0,3,2:T(2,128)(2,1)}, bf16[2,512,12,64]{1,0,3,2:T(2,128)(2,1)S(1)}, u32[]{:S(2)}) copy-start(bf16[2,512,12,64]{1,0,3,2:T(2,128)(2,1)S(1)} %convert_element_type.220) | copy-start | bytes 4718596
  279.8 175.0 %copy-start.59 = (f32[1024]{0:T(1024)}, f32[1024]{0:T(1024)S(1)}, u32[]{:S(2)}) copy-start(f32[1024]{0:T(1024)S(1)} %broadcast_multiply_fusion.10) | copy-start | bytes 12292
  280.3 174.5 %copy-start.67 = (f32[1024]{0:T(1024)}, f32[1024]{0:T(1024)S(1)}, u32[]{:S(2)}) copy-start(f32[1024]{0:T(1024)S(1)} %add_rsqrt_fusion.3) | copy-start | bytes 12292
  335.0 59.2 %copy-start.65 = (f32[768]{0:T(1024)S(1)}, f32[768]{0:T(1024)}, u32[]{:S(2)}) copy-start(f32[768]{0:T(1024)} %convert_element_type.214) | copy-start | bytes 9220
  432.6 22.8 %copy-start.35 = (f32[1024,768]{1,0:T(8,128)S(1)}, f32[1024,768]{1,0:T(8,128)}, u32[]{:S(2)}) copy-start(f32[1024,768]{1,0:T(8,128)} %copy-done.33) | copy-start | bytes 9437188
  534.4 22.4 %copy-start.84 = (bf16[768,768]{1,0:T(8,128)(2,1)S(1)}, bf16[768,768]{1,0:T(8,128)(2,1)}, u32[]{:S(2)}) copy-start(bf16[768,768]{1,0:T(8,128)(2,1)} %all-gather.11.cloned.1.call-done) | copy-start | bytes 3538948
  600.8 22.0 %copy-start.8 = (bf16[2,512,12,64]{1,0,3,2:T(2,128)(2,1)S(1)}, bf16[2,512,12,64]{1,0,3,2:T(2,128)(2,1)}, u32[]{:S(2)}) copy-start(bf16[2,512,12,64]{1,0,3,2:T(2,128)(2,1)} %get-tuple-element.37) | copy-start | bytes 4718596
  685.9 48.4 %copy-start.60 = (f32[1024]{0:T(1024)S(1)}, f32[1024]{0:T(1024)}, u32[]{:S(2)}) copy-start(f32[1024]{0:T(1024)} %copy-done.59) | copy-start | bytes 12292
  685.9 48.4 %copy-start.68 = (f32[1024]{0:T(1024)S(1)}, f32[1024]{0:T(1024)}, u32[]{:S(2)}) copy-start(f32[1024]{0:T(1024)} %copy-done.67) | copy-start | bytes 12292
  685.9 48.4 %copy-start.72 = (f32[1024]{0:T(1024)S(1)}, f32[1024]{0:T(1024)}, u32[]{:S(2)}) copy-start(f32[1024]{0:T(1024)} %copy-done.71) | copy-start | bytes 12292
  685.9 48.4 %copy-start.74 = (f32[1024]{0:T(1024)S(1)}, f32[1024]{0:T(1024)}, u32[]{:S(2)}) copy-start(f32[1024]{0:T(1024)} %copy-done.73) | copy-start | bytes 12292
  690.6 41.7 %copy-start.15 = (bf16[1024,768]{1,0:T(8,128)(2,1)S(1)}, bf16[1024,768]{1,0:T(8,128)(2,1)}, u32[]{:S(2)}) copy-start(bf16[1024,768]{1,0:T(8,128)(2,1)} %get-tuple-element.29) | copy-start | bytes 4718596
  690.6 41.7 %copy-start.16 = (bf16[1024,768]{1,0:T(8,128)(2,1)S(1)}, bf16[1024,768]{1,0:T(8,128)(2,1)}, u32[]{:S(2)}) copy-start(bf16[1024,768]{1,0:T(8,128)(2,1)} %get-tuple-element.30) | copy-start | bytes 4718596
  (63 other events, 418.5 us)
Sparse Core Ops, SparseCore 0:
  26.5 35.4 all-gather.8
  63.9 24.0 all-gather.10
  89.9 38.7 all-gather.12
  130.4 39.6 all-gather.14
